TPU v7x, 256 devices: a whole 4x4x8 slice. The times are simulated.
256 devices in a mesh: blk: 8 (over y, core), sep: 32 (over x, z).
Axes of the slice: x: 4, y: 4, z: 8, core: 2. Of those that a mesh axis runs over, the one named last changes fastest.
Arguments:
- interior_inverse: float32 [8, 32, 1024, 1024], P('blk', 'sep'), as said below
- coupling: float32 [8, 32, 1024, 512], P('blk', 'sep')
- port_matrix: float32 [8, 32, 512, 512], P('blk', 'sep'), as said below
- interior_current: float32 [8, 32, 1024, 128], P('blk', 'sep'), may hold values from -6 to 6
- port_current: float32 [8, 32, 512, 128], P('blk', 'sep'), may hold values from -6 to 6
- port_list: int32 [8, 32, 512], P('blk', 'sep'), may hold values from 0 to 1023, as said below
- spectral_scale: float32 [], replicated, may hold values from 1.5 to 3
Outputs:
- port_voltage: float32 [32, 1024, 128], P('sep', 'blk')
- interior_voltage: float32 [8, 32, 1024, 128], P('blk', 'sep')
Inputs may be any that keep to these rules, and one draw needn't show every extreme that they name: `port_list`: in each block the first 256 entries are distinct, and so are the last ones. Within one separator group, blocks whose b differ by a multiple of 4 name the same sets, and the sets of the first 4 blocks partition the separator's rows, both for the first and for the last halves. `interior_inverse`: symmetric positive definite. Each block's port_matrix minus coupling^T interior_inverse coupling is symmetric positive definite.
All inputs are finite; a program needn't handle non-finite values.
Results may differ from a plain program's by a relative error of at most 0.0001.
Values sent between devices are 32-bit elements; how exact they have to be, the bound alone decides.
No kernel may reach another device: no remote copies, remote signals or barrier semaphores. Data moves between devices by JAX's collectives and lax.ppermute only.
A program may use at most 64 MiB of HBM per device.

v0:
```python
import jax
import jax.numpy as jnp
from jax import lax
from jax.sharding import PartitionSpec as P

SEP_PORTS = 1024
ITERS = 2
DEGREE = 2
HI = lax.Precision.HIGHEST


def shifted(array, axis, by):
    devices = lax.axis_size(axis)
    return lax.ppermute(array, axis, [(i, (i + by) % devices) for i in range(devices)])


def body(
    interior_inverse,
    coupling,
    port_matrix,
    interior_current,
    port_current,
    port_list,
    spectral_scale,
):
    ginv = interior_inverse[0, 0]
    aip = coupling[0, 0]
    app = port_matrix[0, 0]
    inner = interior_current[0, 0]
    outer = port_current[0, 0]
    ports = port_list[0, 0]
    width = aip.shape[1]
    half = width // 2
    lower = ports[:half]
    higher = ports[half:]
    solved = jnp.dot(ginv, jnp.concatenate([aip, inner], axis=1), precision=HI)
    reduced_all = jnp.dot(aip.T, solved, precision=HI)
    schur = app - reduced_all[:, :width]
    reduced = outer - reduced_all[:, width:]

    def spread(owned):
        whole = lax.all_gather(owned, "blk", axis=0, tiled=True)
        after = shifted(whole, "sep", -1)
        return jnp.concatenate([whole[lower], after[higher]], axis=0)

    def split_rows(contrib):
        blank = jnp.zeros((SEP_PORTS, contrib.shape[1]), jnp.float32)
        return (blank.at[lower].add(contrib[:half]), blank.at[higher].add(contrib[half:]))

    def collect(contrib):
        own_part, next_part = split_rows(contrib)
        back = shifted(next_part, "sep", 1)
        return lax.psum_scatter(own_part + back, "blk", scatter_dimension=0, tiled=True)

    diag_column = jnp.diagonal(schur)[:, None]
    own_main, next_main = split_rows(reduced)
    own_diag, next_diag = split_rows(diag_column)
    back_main, back_diag = shifted((next_main, next_diag), "sep", 1)
    rhs, diagonal_sum = (
        lax.psum_scatter(own_main + back_main, "blk", scatter_dimension=0, tiled=True),
        lax.psum_scatter(own_diag + back_diag, "blk", scatter_dimension=0, tiled=True),
    )

    def matvec(vector):
        return collect(jnp.dot(schur, spread(vector), precision=HI))

    def column_sum(left, right):
        return lax.psum(jnp.sum(left * right, axis=0), ("blk", "sep"))

    def precond(residual):
        level = residual / diagonal_sum
        result = level
        for step in range(DEGREE):
            level = level - matvec(level) / (spectral_scale * diagonal_sum)
            result = result + level
        return result

    solution = jnp.zeros_like(rhs)
    residual = rhs
    search = precond(residual)
    direction = search
    inner_rz = column_sum(residual, search)
    for step in range(ITERS):
        image = matvec(direction)
        alpha = inner_rz / column_sum(direction, image)
        solution = solution + alpha * direction
        residual = residual - alpha * image
        if step + 1 < ITERS:
            search = precond(residual)
            newer = column_sum(residual, search)
            direction = search + newer / inner_rz * direction
            inner_rz = newer
    local = spread(solution)
    interior = jnp.dot(ginv, inner - jnp.dot(aip, local, precision=HI), precision=HI)
    return (solution[None], interior[None, None])


def solution(mesh):
    return jax.shard_map(
        body,
        mesh=mesh,
        in_specs=(
            P("blk", "sep", None, None),
            P("blk", "sep", None, None),
            P("blk", "sep", None, None),
            P("blk", "sep", None, None),
            P("blk", "sep", None, None),
            P("blk", "sep", None),
            P(),
        ),
        out_specs=(P("sep", "blk", None), P("blk", "sep", None, None)),
        check_vma=False,
    )
```

profile of v0, /device:TPU:1, one launch (start us, length us, event | category | flops | bytes accessed | tf_op | source)
XLA Modules:
  0.0 939.8 jit_solution(3883574051171454138)
XLA Ops:
  7.9 19.7 %fusion.2 = f32[640,1024]{1,0:T(8,128)S(1)} fusion(f32[1,1,1024,1024]{3,2,1,0:T(8,128)} %param.7, f32[1024,128]{1,0:T(8,128)} %bitcast.56, f32[1024,512]{1,0:T(8,128)} %bitcast.55), kind=kOutput, calls=%fused_computation.33 | convolution fusion | flops 8053719040 | bytes 9437184 | tf_op jit(solution)/shard_map/dot_general | solution.py:36
  65.0 27.5 %reduce-scatter.25.cloned.1.call-done = f32[128,1]{1,0:T(8,128)} async-done(((f32[1024,1]{1,0:T(8,128)}), f32[128,1]{1,0:T(8,128)}) %reduce-scatter.25.cloned.1.call-update) | async-done | bytes 528
  93.4 34.3 %reduce-scatter.11.cloned.1.call-done = f32[128,128]{1,0:T(8,128)} async-done(((f32[1024,128]{1,0:T(8,128)}), f32[128,128]{1,0:T(8,128)}) %reduce-scatter.11.cloned.1.call-update) | async-done | bytes 65552 | tf_op jit(solution)/shard_map/reduce_scatter | solution.py:60
  128.7 17.3 %all_gather.21 = f32[1024,128]{1,0:T(8,128)} all-gather(f32[128,128]{1,0:T(8,128)S(1)} %broadcast_divide_fusion.1), channel_id=1, replica_groups=mesh['blk'=8,'sep'=32] {'blk'}, dimensions={0}, use_global_device_ids=true | all-gather | bytes 589824 | tf_op jit(solution)/shard_map/all_gather | solution.py:42
  170.0 17.1 %collective-permute-done.3 = f32[1024,128]{1,0:T(8,128)} collective-permute-done((f32[1024,128]{1,0:T(8,128)}, f32[1024,128]{1,0:T(8,128)}, u32[]{:S(2)}, u32[]{:S(2)}) %collective-permute-start.3) | collective-permute-done | bytes 524320 | tf_op jit(solution)/shard_map/ppermute | solution.py:14
  191.4 25.9 %reduce-scatter.13.cloned.1.call-done = f32[128,128]{1,0:T(8,128)} async-done(((f32[1024,128]{1,0:T(8,128)}), f32[128,128]{1,0:T(8,128)}) %reduce-scatter.13.cloned.1.call-update) | async-done | bytes 65552 | tf_op jit(solution)/shard_map/reduce_scatter | solution.py:53
  218.3 16.9 %all_gather.22 = f32[1024,128]{1,0:T(8,128)} all-gather(f32[128,128]{1,0:T(8,128)S(1)} %divide_subtract_fusion.1), channel_id=1, replica_groups=mesh['blk'=8,'sep'=32] {'blk'}, dimensions={0}, use_global_device_ids=true | all-gather | bytes 589824 | tf_op jit(solution)/shard_map/all_gather | solution.py:42
  259.5 17.1 %collective-permute-done.5 = f32[1024,128]{1,0:T(8,128)} collective-permute-done((f32[1024,128]{1,0:T(8,128)}, f32[1024,128]{1,0:T(8,128)}, u32[]{:S(2)}, u32[]{:S(2)}) %collective-permute-start.5) | collective-permute-done | bytes 524320 | tf_op jit(solution)/shard_map/ppermute | solution.py:14
  280.2 26.6 %reduce-scatter.15.cloned.1.call-done = f32[128,128]{1,0:T(8,128)} async-done(((f32[1024,128]{1,0:T(8,128)}), f32[128,128]{1,0:T(8,128)}) %reduce-scatter.15.cloned.1.call-update) | async-done | bytes 65552 | tf_op jit(solution)/shard_map/reduce_scatter | solution.py:53
  307.8 16.9 %all_gather.23 = f32[1024,128]{1,0:T(8,128)} all-gather(f32[128,128]{1,0:T(8,128)S(1)} %subtract_add_fusion.1), channel_id=1, replica_groups=mesh['blk'=8,'sep'=32] {'blk'}, dimensions={0}, use_global_device_ids=true | all-gather | bytes 589824 | tf_op jit(solution)/shard_map/all_gather | solution.py:42
  348.8 17.1 %collective-permute-done.7 = f32[1024,128]{1,0:T(8,128)} collective-permute-done((f32[1024,128]{1,0:T(8,128)}, f32[1024,128]{1,0:T(8,128)}, u32[]{:S(2)}, u32[]{:S(2)}) %collective-permute-start.7) | collective-permute-done | bytes 524320 | tf_op jit(solution)/shard_map/ppermute | solution.py:14
  369.6 26.6 %reduce-scatter.17.cloned.1.call-done = f32[128,128]{1,0:T(8,128)} async-done(((f32[1024,128]{1,0:T(8,128)}), f32[128,128]{1,0:T(8,128)}) %reduce-scatter.17.cloned.1.call-update) | async-done | bytes 65552 | tf_op jit(solution)/shard_map/reduce_scatter | solution.py:53
  397.1 78.2 %all-reduce = (f32[128]{0:T(128)S(1)}, f32[128]{0:T(128)S(1)}) all-reduce(f32[128]{0:T(128)S(1)} %get-tuple-element.9, f32[128]{0:T(128)S(1)} %get-tuple-element.8), channel_id=1, replica_groups=mesh['blk'=8,'sep'=32] {'blk','sep'}, use_global_device_ids=true, to_apply=%region_13.14 | all-reduce | flops 256 | bytes 2048 | tf_op jit(solution)/shard_map/psum | solution.py:68
  476.8 14.9 %all_gather.24 = f32[1024,128]{1,0:T(8,128)} all-gather(f32[128,128]{1,0:T(8,128)S(1)} %broadcast_divide_fusion), channel_id=1, replica_groups=mesh['blk'=8,'sep'=32] {'blk'}, dimensions={0}, use_global_device_ids=true | all-gather | bytes 589824 | tf_op jit(solution)/shard_map/all_gather | solution.py:42
  515.0 15.9 %collective-permute-done.9 = f32[1024,128]{1,0:T(8,128)} collective-permute-done((f32[1024,128]{1,0:T(8,128)}, f32[1024,128]{1,0:T(8,128)}, u32[]{:S(2)}, u32[]{:S(2)}) %collective-permute-start.9) | collective-permute-done | bytes 524320 | tf_op jit(solution)/shard_map/ppermute | solution.py:14
  534.9 26.6 %reduce-scatter.19.cloned.1.call-done = f32[128,128]{1,0:T(8,128)} async-done(((f32[1024,128]{1,0:T(8,128)}), f32[128,128]{1,0:T(8,128)}) %reduce-scatter.19.cloned.1.call-update) | async-done | bytes 65552 | tf_op jit(solution)/shard_map/reduce_scatter | solution.py:53
  562.4 16.9 %all_gather.25 = f32[1024,128]{1,0:T(8,128)} all-gather(f32[128,128]{1,0:T(8,128)S(1)} %divide_subtract_fusion), channel_id=1, replica_groups=mesh['blk'=8,'sep'=32] {'blk'}, dimensions={0}, use_global_device_ids=true | all-gather | bytes 589824 | tf_op jit(solution)/shard_map/all_gather | solution.py:42
  604.3 17.1 %collective-permute-done.11 = f32[1024,128]{1,0:T(8,128)} collective-permute-done((f32[1024,128]{1,0:T(8,128)}, f32[1024,128]{1,0:T(8,128)}, u32[]{:S(2)}, u32[]{:S(2)}) %collective-permute-start.11) | collective-permute-done | bytes 524320 | tf_op jit(solution)/shard_map/ppermute | solution.py:14
  625.4 26.5 %reduce-scatter.21.cloned.1.call-done = f32[128,128]{1,0:T(8,128)} async-done(((f32[1024,128]{1,0:T(8,128)}), f32[128,128]{1,0:T(8,128)}) %reduce-scatter.21.cloned.1.call-update) | async-done | bytes 65552 | tf_op jit(solution)/shard_map/reduce_scatter | solution.py:53
  652.9 78.3 %psum.30 = f32[128]{0:T(128)S(1)} all-reduce(f32[128]{0:T(128)S(1)} %get-tuple-element.12), channel_id=1, replica_groups=mesh['blk'=8,'sep'=32] {'blk','sep'}, use_global_device_ids=true, to_apply=%region_26.27 | all-reduce | flops 128 | bytes 1024 | tf_op jit(solution)/shard_map/psum | solution.py:68
  731.8 15.2 %all_gather.26 = f32[1024,128]{1,0:T(8,128)} all-gather(f32[128,128]{1,0:T(8,128)S(1)} %multiply_add_fusion.1), channel_id=1, replica_groups=mesh['blk'=8,'sep'=32] {'blk'}, dimensions={0}, use_global_device_ids=true | all-gather | bytes 589824 | tf_op jit(solution)/shard_map/all_gather | solution.py:42
  768.5 15.5 %collective-permute-done.13 = f32[1024,128]{1,0:T(8,128)S(1)} collective-permute-done((f32[1024,128]{1,0:T(8,128)S(1)}, f32[1024,128]{1,0:T(8,128)S(1)}, u32[]{:S(2)}, u32[]{:S(2)}) %collective-permute-start.13) | collective-permute-done | bytes 524320 | tf_op jit(solution)/shard_map/ppermute | solution.py:14
  787.0 26.6 %reduce-scatter.23.cloned.1.call-done = f32[128,128]{1,0:T(8,128)} async-done(((f32[1024,128]{1,0:T(8,128)}), f32[128,128]{1,0:T(8,128)}) %reduce-scatter.23.cloned.1.call-update) | async-done | bytes 65552 | tf_op jit(solution)/shard_map/reduce_scatter | solution.py:53
  814.5 78.2 %psum.31 = f32[128]{0:T(128)S(1)} all-reduce(f32[128]{0:T(128)S(1)} %multiply_reduce_fusion), channel_id=1, replica_groups=mesh['blk'=8,'sep'=32] {'blk','sep'}, use_global_device_ids=true, to_apply=%region_31.32 | all-reduce | flops 128 | bytes 1024 | tf_op jit(solution)/shard_map/psum | solution.py:68
  (139 shorter events, 251.2 us)
Async XLA Ops:
  7.2 85.4 %reduce-scatter.25.cloned.1.call-start = ((), (), s32[]{:S(2)}) async-start(), calls=%async_computation.15 | async-start | bytes 589824
  7.9 159.8 %copy-start.11 = (s32[256,1]{0,1:T(1,128)}, s32[256,1]{0,1:T(1,128)S(1)}, u32[]{:S(2)}) copy-start(s32[256,1]{0,1:T(1,128)S(1)} %get-tuple-element.19) | copy-start | bytes 3076
  36.5 24.8 %collective-permute-start = (f32[1024,128]{1,0:T(8,128)}, f32[1024,128]{1,0:T(8,128)}, u32[]{:S(2)}, u32[]{:S(2)}) collective-permute-start(f32[1024,128]{1,0:T(8,128)} %scatter_custom_fusion), channel_id=1, source_target_pairs={{0,1},{1,2},{2,3},{3,4},{4,5},{5,6},{6,7},{7,8},{8,9},{9,10},{10,1... | collective-permute-start | bytes 1572872 | tf_op jit(solution)/shard_map/ppermute | solution.py:14
  50.1 7.7 collective-permute-start.1
  61.1 66.6 %reduce-scatter.11.cloned.1.call-start = ((), (), s32[]{:S(2)}) async-start(), calls=%async_computation.8 | async-start | bytes 589824 | tf_op jit(solution)/shard_map/reduce_scatter | solution.py:60
  64.9 152.4 %reduce-scatter.13.cloned.1.call-start = ((), (), s32[]{:S(2)}) async-start(), calls=%async_computation.9 | async-start | bytes 589824 | tf_op jit(solution)/shard_map/reduce_scatter | solution.py:53
  146.0 16.6 %collective-permute-start.2 = (f32[1024,128]{1,0:T(8,128)}, f32[1024,128]{1,0:T(8,128)}, u32[]{:S(2)}, u32[]{:S(2)}) collective-permute-start(f32[1024,128]{1,0:T(8,128)} %all_gather.21), channel_id=1, source_target_pairs={{0,31},{1,0},{2,1},{3,2},{4,3},{5,4},{6,5},{7,6},{8,7},{9,8},{10,9... | collective-permute-start | bytes 1572872 | tf_op jit(solution)/shard_map/ppermute | solution.py:14
  170.0 17.1 %collective-permute-start.3 = (f32[1024,128]{1,0:T(8,128)}, f32[1024,128]{1,0:T(8,128)}, u32[]{:S(2)}, u32[]{:S(2)}) collective-permute-start(f32[1024,128]{1,0:T(8,128)} %scatter_custom_fusion.4), channel_id=1, source_target_pairs={{0,1},{1,2},{2,3},{3,4},{4,5},{5,6},{6,7},{7,8},{8,9},{9,10},{10,1... | collective-permute-start | bytes 1572872 | tf_op jit(solution)/shard_map/ppermute | solution.py:14
  190.7 116.1 %reduce-scatter.15.cloned.1.call-start = ((), (), s32[]{:S(2)}) async-start(), calls=%async_computation.10 | async-start | bytes 589824 | tf_op jit(solution)/shard_map/reduce_scatter | solution.py:53
  235.2 16.6 %collective-permute-start.4 = (f32[1024,128]{1,0:T(8,128)}, f32[1024,128]{1,0:T(8,128)}, u32[]{:S(2)}, u32[]{:S(2)}) collective-permute-start(f32[1024,128]{1,0:T(8,128)} %all_gather.22), channel_id=1, source_target_pairs={{0,31},{1,0},{2,1},{3,2},{4,3},{5,4},{6,5},{7,6},{8,7},{9,8},{10,9... | collective-permute-start | bytes 1572872 | tf_op jit(solution)/shard_map/ppermute | solution.py:14
  259.3 17.3 %collective-permute-start.5 = (f32[1024,128]{1,0:T(8,128)}, f32[1024,128]{1,0:T(8,128)}, u32[]{:S(2)}, u32[]{:S(2)}) collective-permute-start(f32[1024,128]{1,0:T(8,128)} %scatter_custom_fusion.6), channel_id=1, source_target_pairs={{0,1},{1,2},{2,3},{3,4},{4,5},{5,6},{6,7},{7,8},{8,9},{9,10},{10,1... | collective-permute-start | bytes 1572872 | tf_op jit(solution)/shard_map/ppermute | solution.py:14
  280.2 116.0 %reduce-scatter.17.cloned.1.call-start = ((), (), s32[]{:S(2)}) async-start(), calls=%async_computation.11 | async-start | bytes 589824 | tf_op jit(solution)/shard_map/reduce_scatter | solution.py:53
  324.7 16.6 %collective-permute-start.6 = (f32[1024,128]{1,0:T(8,128)}, f32[1024,128]{1,0:T(8,128)}, u32[]{:S(2)}, u32[]{:S(2)}) collective-permute-start(f32[1024,128]{1,0:T(8,128)} %all_gather.23), channel_id=1, source_target_pairs={{0,31},{1,0},{2,1},{3,2},{4,3},{5,4},{6,5},{7,6},{8,7},{9,8},{10,9... | collective-permute-start | bytes 1572872 | tf_op jit(solution)/shard_map/ppermute | solution.py:14
  348.8 17.1 %collective-permute-start.7 = (f32[1024,128]{1,0:T(8,128)}, f32[1024,128]{1,0:T(8,128)}, u32[]{:S(2)}, u32[]{:S(2)}) collective-permute-start(f32[1024,128]{1,0:T(8,128)} %scatter_custom_fusion.8), channel_id=1, source_target_pairs={{0,1},{1,2},{2,3},{3,4},{4,5},{5,6},{6,7},{7,8},{8,9},{9,10},{10,1... | collective-permute-start | bytes 1572872 | tf_op jit(solution)/shard_map/ppermute | solution.py:14
  369.6 191.9 %reduce-scatter.19.cloned.1.call-start = ((), (), s32[]{:S(2)}) async-start(), calls=%async_computation.12 | async-start | bytes 589824 | tf_op jit(solution)/shard_map/reduce_scatter | solution.py:53
  491.7 14.0 %collective-permute-start.8 = (f32[1024,128]{1,0:T(8,128)}, f32[1024,128]{1,0:T(8,128)}, u32[]{:S(2)}, u32[]{:S(2)}) collective-permute-start(f32[1024,128]{1,0:T(8,128)} %all_gather.24), channel_id=1, source_target_pairs={{0,31},{1,0},{2,1},{3,2},{4,3},{5,4},{6,5},{7,6},{8,7},{9,8},{10,9... | collective-permute-start | bytes 1572872 | tf_op jit(solution)/shard_map/ppermute | solution.py:14
  514.0 16.8 %collective-permute-start.9 = (f32[1024,128]{1,0:T(8,128)}, f32[1024,128]{1,0:T(8,128)}, u32[]{:S(2)}, u32[]{:S(2)}) collective-permute-start(f32[1024,128]{1,0:T(8,128)} %scatter_custom_fusion.10), channel_id=1, source_target_pairs={{0,1},{1,2},{2,3},{3,4},{4,5},{5,6},{6,7},{7,8},{8,9},{9,10},{10,1... | collective-permute-start | bytes 1572872 | tf_op jit(solution)/shard_map/ppermute | solution.py:14
  534.8 117.1 %reduce-scatter.21.cloned.1.call-start = ((), (), s32[]{:S(2)}) async-start(), calls=%async_computation.13 | async-start | bytes 589824 | tf_op jit(solution)/shard_map/reduce_scatter | solution.py:53
  579.3 16.6 %collective-permute-start.10 = (f32[1024,128]{1,0:T(8,128)}, f32[1024,128]{1,0:T(8,128)}, u32[]{:S(2)}, u32[]{:S(2)}) collective-permute-start(f32[1024,128]{1,0:T(8,128)} %all_gather.25), channel_id=1, source_target_pairs={{0,31},{1,0},{2,1},{3,2},{4,3},{5,4},{6,5},{7,6},{8,7},{9,8},{10,9... | collective-permute-start | bytes 1572872 | tf_op jit(solution)/shard_map/ppermute | solution.py:14
  604.3 17.1 %collective-permute-start.11 = (f32[1024,128]{1,0:T(8,128)}, f32[1024,128]{1,0:T(8,128)}, u32[]{:S(2)}, u32[]{:S(2)}) collective-permute-start(f32[1024,128]{1,0:T(8,128)} %scatter_custom_fusion.12), channel_id=1, source_target_pairs={{0,1},{1,2},{2,3},{3,4},{4,5},{5,6},{6,7},{7,8},{8,9},{9,10},{10,1... | collective-permute-start | bytes 1572872 | tf_op jit(solution)/shard_map/ppermute | solution.py:14
  625.4 188.2 %reduce-scatter.23.cloned.1.call-start = ((), (), s32[]{:S(2)}) async-start(), calls=%async_computation.14 | async-start | bytes 589824 | tf_op jit(solution)/shard_map/reduce_scatter | solution.py:53
  747.0 13.6 %collective-permute-start.12 = (f32[1024,128]{1,0:T(8,128)}, f32[1024,128]{1,0:T(8,128)}, u32[]{:S(2)}, u32[]{:S(2)}) collective-permute-start(f32[1024,128]{1,0:T(8,128)} %all_gather.26), channel_id=1, source_target_pairs={{0,31},{1,0},{2,1},{3,2},{4,3},{5,4},{6,5},{7,6},{8,7},{9,8},{10,9... | collective-permute-start | bytes 1572872 | tf_op jit(solution)/shard_map/ppermute | solution.py:14
  767.5 16.5 %collective-permute-start.13 = (f32[1024,128]{1,0:T(8,128)S(1)}, f32[1024,128]{1,0:T(8,128)S(1)}, u32[]{:S(2)}, u32[]{:S(2)}) collective-permute-start(f32[1024,128]{1,0:T(8,128)S(1)} %scatter_custom_fusion.14), channel_id=1, source_target_pairs={{0,1},{1,2},{2,3},{3,4},{4,5},{5,6},{6,7},{7,8},{8,9},{9,10},{10,1... | collective-permute-start | bytes 1572872 | tf_op jit(solution)/shard_map/ppermute | solution.py:14
  907.2 13.6 %collective-permute-start.14 = (f32[1024,128]{1,0:T(8,128)S(1)}, f32[1024,128]{1,0:T(8,128)S(1)}, u32[]{:S(2)}, u32[]{:S(2)}) collective-permute-start(f32[1024,128]{1,0:T(8,128)S(1)} %all_gather.27), channel_id=1, source_target_pairs={{0,31},{1,0},{2,1},{3,2},{4,3},{5,4},{6,5},{7,6},{8,7},{9,8},{10,9... | collective-permute-start | bytes 1572872 | tf_op jit(solution)/shard_map/ppermute | solution.py:14
  (13 other events, 586.0 us)
Sparse Core Ops, SparseCore 0:
  61.3 31.2 reduce-scatter.24
  95.0 32.6 reduce-scatter.10
  190.8 26.4 reduce-scatter.12
  280.3 26.4 reduce-scatter.14
  369.7 26.4 reduce-scatter.16
  535.0 26.4 reduce-scatter.18
  625.5 26.3 reduce-scatter.20
  787.1 26.4 reduce-scatter.22
where the time goes:
time: 948 us; the launch traced here: 940 us
  waiting for transfers between devices  391 us (41%)
  blocking collectives  347 us (37%)
  other arithmetic  57.1 us (6%)
  matrix products  52.9 us (6%)
  local copies, waits for them, and re-layouts  42.7 us (5%)
  starting transfers between devices  33.4 us (4%)
  between operations  15.6 us (2%)
    psum x3, blocking collectives, column_sum(): return lax.psum(jnp.sum(left * right, axis=0), ('blk', 'sep'))  235 us
    ppermute x15, waiting for transfers between devices, shifted(): lax.ppermute(array, axis, [(i, (i + by) % devices) for i in range(devices)])  171 us
    reduce_scatter x6, waiting for transfers between devices, collect(): lax.psum_scatter(own_part + back, 'blk', scatter_dimension=0, tiled=True)  159 us
    all_gather x7, blocking collectives, spread(): whole = lax.all_gather(owned, 'blk', axis=0, tiled=True)  112 us
    reduce_scatter x1, waiting for transfers between devices, body(): lax.psum_scatter(own_main + back_main, 'blk', scatter_dimension=0, tiled=...  34.3 us
    ppermute x15, starting transfers between devices, shifted(): lax.ppermute(array, axis, [(i, (i + by) % devices) for i in range(devices)])  33 us
    gather x14, local copies, waits for them, and re-layouts, spread(): return jnp.concatenate([whole[lower], after[higher]], axis=0)  29 us
    unnamed x9, waiting for transfers between devices  27.7 us
  transfers between devices with their start and end apart: 23, of which 22 were waited for; matrix products, arithmetic and copies ran while one was open for 4% of the time, Pallas kernels for 0%

commit v1 on v0

--- a/solution.py
+++ b/solution.py
@@ -7,6 +7,11 @@
 ITERS = 2
 DEGREE = 2
 HI = lax.Precision.HIGHEST
+
+
+def tiled_gather(x, axis, dim):
+    copies = jnp.concatenate([x] * lax.axis_size(axis), axis=dim)
+    return lax.all_to_all(copies, axis, dim, dim, tiled=True)
 
 
 def shifted(array, axis, by):
@@ -39,7 +44,7 @@
     reduced = outer - reduced_all[:, width:]
 
     def spread(owned):
-        whole = lax.all_gather(owned, "blk", axis=0, tiled=True)
+        whole = tiled_gather(owned, "blk", 0)
         after = shifted(whole, "sep", -1)
         return jnp.concatenate([whole[lower], after[higher]], axis=0)
 

time: 948 us -> 938 us (0.989)
  blocking collectives: 347 us -> 335 us
    all_gather x7 -> x0, blocking collectives: 112 us -> none  [spread(): whole = lax.all_gather(owned, 'blk', axis=0, tiled=True)]
    all_to_all x0 -> x7, blocking collectives: none -> 101 us  [tiled_gather(): return lax.all_to_all(copies, axis, dim, dim, tiled=True)]
    ppermute x15, waiting for transfers between devices: 171 us -> 159 us  [shifted(): lax.ppermute(array, axis, [(i, (i + by) % devices) for i in range(devices)])]
    unnamed x0 -> x13, other arithmetic: none -> 10.3 us
where the time goes in v1:
time: 938 us; the launch traced here: 930 us
  waiting for transfers between devices  383 us (41%)
  blocking collectives  335 us (36%)
  other arithmetic  65 us (7%)
  matrix products  53.6 us (6%)
  local copies, waits for them, and re-layouts  43 us (5%)
  starting transfers between devices  33.5 us (4%)
  between operations  15.9 us (2%)
    psum x3, blocking collectives, column_sum(): return lax.psum(jnp.sum(left * right, axis=0), ('blk', 'sep'))  235 us
    reduce_scatter x6, waiting for transfers between devices, collect(): lax.psum_scatter(own_part + back, 'blk', scatter_dimension=0, tiled=True)  162 us
    ppermute x15, waiting for transfers between devices, shifted(): lax.ppermute(array, axis, [(i, (i + by) % devices) for i in range(devices)])  159 us
    all_to_all x7, blocking collectives, tiled_gather(): return lax.all_to_all(copies, axis, dim, dim, tiled=True)  101 us
    reduce_scatter x1, waiting for transfers between devices, body(): lax.psum_scatter(own_main + back_main, 'blk', scatter_dimension=0, tiled=...  34.3 us
    ppermute x15, starting transfers between devices, shifted(): lax.ppermute(array, axis, [(i, (i + by) % devices) for i in range(devices)])  33.2 us
    gather x14, local copies, waits for them, and re-layouts, spread(): return jnp.concatenate([whole[lower], after[higher]], axis=0)  29 us
    unnamed x9, waiting for transfers between devices  27.7 us
  transfers between devices with their start and end apart: 23, of which 22 were waited for; matrix products, arithmetic and copies ran while one was open for 4% of the time, Pallas kernels for 0%

profile of v1, /device:TPU:1, one launch (start us, length us, event | category | flops | bytes accessed | tf_op | source)
XLA Modules:
  0.0 929.7 jit_solution(4796296511614965544)
XLA Ops:
  7.9 19.7 %fusion.2 = f32[640,1024]{1,0:T(8,128)S(1)} fusion(f32[1,1,1024,1024]{3,2,1,0:T(8,128)} %param.7, f32[1024,128]{1,0:T(8,128)} %bitcast.80, f32[1024,512]{1,0:T(8,128)} %bitcast.69), kind=kOutput, calls=%fused_computation.33 | convolution fusion | flops 8053719040 | bytes 9437184 | tf_op jit(solution)/shard_map/dot_general | solution.py:41
  65.0 27.5 %reduce-scatter.25.cloned.1.call-done = f32[128,1]{1,0:T(8,128)} async-done(((f32[1024,1]{1,0:T(8,128)}), f32[128,1]{1,0:T(8,128)}) %reduce-scatter.25.cloned.1.call-update) | async-done | bytes 528
  93.4 34.3 %reduce-scatter.11.cloned.1.call-done = f32[128,128]{1,0:T(8,128)} async-done(((f32[1024,128]{1,0:T(8,128)}), f32[128,128]{1,0:T(8,128)}) %reduce-scatter.11.cloned.1.call-update) | async-done | bytes 65552 | tf_op jit(solution)/shard_map/reduce_scatter | solution.py:65
  135.2 15.3 %all_to_all.84 = f32[8,128,128]{2,1,0:T(8,128)} all-to-all(f32[8,128,128]{2,1,0:T(8,128)S(1)} %bitcast.74), channel_id=1, replica_groups=mesh['blk'=8,'sep'=32] {'blk'}, dimensions={0} | all-to-all | bytes 1048576 | tf_op jit(solution)/shard_map/all_to_all | solution.py:14
  174.1 16.2 %collective-permute-done.3 = f32[1024,128]{1,0:T(8,128)} collective-permute-done((f32[1024,128]{1,0:T(8,128)}, f32[1024,128]{1,0:T(8,128)}, u32[]{:S(2)}, u32[]{:S(2)}) %collective-permute-start.3) | collective-permute-done | bytes 524320 | tf_op jit(solution)/shard_map/ppermute | solution.py:19
  194.7 26.5 %reduce-scatter.13.cloned.1.call-done = f32[128,128]{1,0:T(8,128)} async-done(((f32[1024,128]{1,0:T(8,128)}), f32[128,128]{1,0:T(8,128)}) %reduce-scatter.13.cloned.1.call-update) | async-done | bytes 65552 | tf_op jit(solution)/shard_map/reduce_scatter | solution.py:58
  222.2 15.3 %all_to_all.85 = f32[8,128,128]{2,1,0:T(8,128)} all-to-all(f32[8,128,128]{2,1,0:T(8,128)S(1)} %bitcast.77), channel_id=1, replica_groups=mesh['blk'=8,'sep'=32] {'blk'}, dimensions={0} | all-to-all | bytes 1048576 | tf_op jit(solution)/shard_map/all_to_all | solution.py:14
  261.6 16.2 %collective-permute-done.5 = f32[1024,128]{1,0:T(8,128)} collective-permute-done((f32[1024,128]{1,0:T(8,128)}, f32[1024,128]{1,0:T(8,128)}, u32[]{:S(2)}, u32[]{:S(2)}) %collective-permute-start.5) | collective-permute-done | bytes 524320 | tf_op jit(solution)/shard_map/ppermute | solution.py:19
  281.9 27.2 %reduce-scatter.15.cloned.1.call-done = f32[128,128]{1,0:T(8,128)} async-done(((f32[1024,128]{1,0:T(8,128)}), f32[128,128]{1,0:T(8,128)}) %reduce-scatter.15.cloned.1.call-update) | async-done | bytes 65552 | tf_op jit(solution)/shard_map/reduce_scatter | solution.py:58
  310.2 15.3 %all_to_all.86 = f32[8,128,128]{2,1,0:T(8,128)} all-to-all(f32[8,128,128]{2,1,0:T(8,128)S(1)} %bitcast.73), channel_id=1, replica_groups=mesh['blk'=8,'sep'=32] {'blk'}, dimensions={0} | all-to-all | bytes 1048576 | tf_op jit(solution)/shard_map/all_to_all | solution.py:14
  348.8 16.2 %collective-permute-done.7 = f32[1024,128]{1,0:T(8,128)} collective-permute-done((f32[1024,128]{1,0:T(8,128)}, f32[1024,128]{1,0:T(8,128)}, u32[]{:S(2)}, u32[]{:S(2)}) %collective-permute-start.7) | collective-permute-done | bytes 524320 | tf_op jit(solution)/shard_map/ppermute | solution.py:19
  368.7 27.1 %reduce-scatter.17.cloned.1.call-done = f32[128,128]{1,0:T(8,128)} async-done(((f32[1024,128]{1,0:T(8,128)}), f32[128,128]{1,0:T(8,128)}) %reduce-scatter.17.cloned.1.call-update) | async-done | bytes 65552 | tf_op jit(solution)/shard_map/reduce_scatter | solution.py:58
  396.8 78.2 %all-reduce = (f32[128]{0:T(128)S(1)}, f32[128]{0:T(128)S(1)}) all-reduce(f32[128]{0:T(128)S(1)} %get-tuple-element.9, f32[128]{0:T(128)S(1)} %get-tuple-element.8), channel_id=1, replica_groups=mesh['blk'=8,'sep'=32] {'blk','sep'}, use_global_device_ids=true, to_apply=%region_13.14 | all-reduce | flops 256 | bytes 2048 | tf_op jit(solution)/shard_map/psum | solution.py:73
  476.6 13.3 %all_to_all.87 = f32[8,128,128]{2,1,0:T(8,128)} all-to-all(f32[8,128,128]{2,1,0:T(8,128)S(1)} %bitcast.78), channel_id=1, replica_groups=mesh['blk'=8,'sep'=32] {'blk'}, dimensions={0} | all-to-all | bytes 1048576 | tf_op jit(solution)/shard_map/all_to_all | solution.py:14
  512.0 14.9 %collective-permute-done.9 = f32[1024,128]{1,0:T(8,128)} collective-permute-done((f32[1024,128]{1,0:T(8,128)}, f32[1024,128]{1,0:T(8,128)}, u32[]{:S(2)}, u32[]{:S(2)}) %collective-permute-start.9) | collective-permute-done | bytes 524320 | tf_op jit(solution)/shard_map/ppermute | solution.py:19
  530.9 27.2 %reduce-scatter.19.cloned.1.call-done = f32[128,128]{1,0:T(8,128)} async-done(((f32[1024,128]{1,0:T(8,128)}), f32[128,128]{1,0:T(8,128)}) %reduce-scatter.19.cloned.1.call-update) | async-done | bytes 65552 | tf_op jit(solution)/shard_map/reduce_scatter | solution.py:58
  559.1 15.3 %all_to_all.88 = f32[8,128,128]{2,1,0:T(8,128)} all-to-all(f32[8,128,128]{2,1,0:T(8,128)S(1)} %bitcast.79), channel_id=1, replica_groups=mesh['blk'=8,'sep'=32] {'blk'}, dimensions={0} | all-to-all | bytes 1048576 | tf_op jit(solution)/shard_map/all_to_all | solution.py:14
  598.8 16.2 %collective-permute-done.11 = f32[1024,128]{1,0:T(8,128)} collective-permute-done((f32[1024,128]{1,0:T(8,128)}, f32[1024,128]{1,0:T(8,128)}, u32[]{:S(2)}, u32[]{:S(2)}) %collective-permute-start.11) | collective-permute-done | bytes 524320 | tf_op jit(solution)/shard_map/ppermute | solution.py:19
  619.1 27.2 %reduce-scatter.21.cloned.1.call-done = f32[128,128]{1,0:T(8,128)} async-done(((f32[1024,128]{1,0:T(8,128)}), f32[128,128]{1,0:T(8,128)}) %reduce-scatter.21.cloned.1.call-update) | async-done | bytes 65552 | tf_op jit(solution)/shard_map/reduce_scatter | solution.py:58
  647.7 78.3 %psum.30 = f32[128]{0:T(128)S(1)} all-reduce(f32[128]{0:T(128)} %get-tuple-element.16), channel_id=1, replica_groups=mesh['blk'=8,'sep'=32] {'blk','sep'}, use_global_device_ids=true, to_apply=%region_26.27 | all-reduce | flops 128 | bytes 1024 | tf_op jit(solution)/shard_map/psum | solution.py:73
  726.7 13.3 %all_to_all.89 = f32[8,128,128]{2,1,0:T(8,128)} all-to-all(f32[8,128,128]{2,1,0:T(8,128)S(1)} %bitcast.76), channel_id=1, replica_groups=mesh['blk'=8,'sep'=32] {'blk'}, dimensions={0} | all-to-all | bytes 1048576 | tf_op jit(solution)/shard_map/all_to_all | solution.py:14
  760.7 14.6 %collective-permute-done.13 = f32[1024,128]{1,0:T(8,128)S(1)} collective-permute-done((f32[1024,128]{1,0:T(8,128)S(1)}, f32[1024,128]{1,0:T(8,128)S(1)}, u32[]{:S(2)}, u32[]{:S(2)}) %collective-permute-start.13) | collective-permute-done | bytes 524320 | tf_op jit(solution)/shard_map/ppermute | solution.py:19
  778.5 27.2 %reduce-scatter.23.cloned.1.call-done = f32[128,128]{1,0:T(8,128)} async-done(((f32[1024,128]{1,0:T(8,128)}), f32[128,128]{1,0:T(8,128)}) %reduce-scatter.23.cloned.1.call-update) | async-done | bytes 65552 | tf_op jit(solution)/shard_map/reduce_scatter | solution.py:58
  806.6 78.2 %psum.31 = f32[128]{0:T(128)S(1)} all-reduce(f32[128]{0:T(128)S(1)} %multiply_reduce_fusion), channel_id=1, replica_groups=mesh['blk'=8,'sep'=32] {'blk','sep'}, use_global_device_ids=true, to_apply=%region_31.32 | all-reduce | flops 128 | bytes 1024 | tf_op jit(solution)/shard_map/psum | solution.py:73
  (186 shorter events, 252.8 us)
Async XLA Ops:
  7.2 85.4 %reduce-scatter.25.cloned.1.call-start = ((), (), s32[]{:S(2)}) async-start(), calls=%async_computation.22 | async-start | bytes 589824
  7.9 251.2 %copy-start.10 = (s32[256,1]{0,1:T(1,128)}, s32[256,1]{0,1:T(1,128)S(1)}, u32[]{:S(2)}) copy-start(s32[256,1]{0,1:T(1,128)S(1)} %get-tuple-element.31) | copy-start | bytes 3076
  36.5 24.8 %collective-permute-start = (f32[1024,128]{1,0:T(8,128)}, f32[1024,128]{1,0:T(8,128)}, u32[]{:S(2)}, u32[]{:S(2)}) collective-permute-start(f32[1024,128]{1,0:T(8,128)} %scatter_custom_fusion), channel_id=1, source_target_pairs={{0,1},{1,2},{2,3},{3,4},{4,5},{5,6},{6,7},{7,8},{8,9},{9,10},{10,1... | collective-permute-start | bytes 1572872 | tf_op jit(solution)/shard_map/ppermute | solution.py:19
  50.1 7.7 collective-permute-start.1
  61.2 66.6 %reduce-scatter.11.cloned.1.call-start = ((), (), s32[]{:S(2)}) async-start(), calls=%async_computation.15 | async-start | bytes 589824 | tf_op jit(solution)/shard_map/reduce_scatter | solution.py:65
  64.9 156.2 %reduce-scatter.13.cloned.1.call-start = ((), (), s32[]{:S(2)}) async-start(), calls=%async_computation.16 | async-start | bytes 589824 | tf_op jit(solution)/shard_map/reduce_scatter | solution.py:58
  150.5 16.2 %collective-permute-start.2 = (f32[1024,128]{1,0:T(8,128)}, f32[1024,128]{1,0:T(8,128)}, u32[]{:S(2)}, u32[]{:S(2)}) collective-permute-start(f32[1024,128]{1,0:T(8,128)} %bitcast.17), channel_id=1, source_target_pairs={{0,31},{1,0},{2,1},{3,2},{4,3},{5,4},{6,5},{7,6},{8,7},{9,8},{10,9... | collective-permute-start | bytes 1572872 | tf_op jit(solution)/shard_map/ppermute | solution.py:19
  174.1 16.2 %collective-permute-start.3 = (f32[1024,128]{1,0:T(8,128)}, f32[1024,128]{1,0:T(8,128)}, u32[]{:S(2)}, u32[]{:S(2)}) collective-permute-start(f32[1024,128]{1,0:T(8,128)} %scatter_custom_fusion.4), channel_id=1, source_target_pairs={{0,1},{1,2},{2,3},{3,4},{4,5},{5,6},{6,7},{7,8},{8,9},{9,10},{10,1... | collective-permute-start | bytes 1572872 | tf_op jit(solution)/shard_map/ppermute | solution.py:19
  194.0 115.1 %reduce-scatter.15.cloned.1.call-start = ((), (), s32[]{:S(2)}) async-start(), calls=%async_computation.17 | async-start | bytes 589824 | tf_op jit(solution)/shard_map/reduce_scatter | solution.py:58
  237.6 15.7 %collective-permute-start.4 = (f32[1024,128]{1,0:T(8,128)}, f32[1024,128]{1,0:T(8,128)}, u32[]{:S(2)}, u32[]{:S(2)}) collective-permute-start(f32[1024,128]{1,0:T(8,128)} %bitcast.20), channel_id=1, source_target_pairs={{0,31},{1,0},{2,1},{3,2},{4,3},{5,4},{6,5},{7,6},{8,7},{9,8},{10,9... | collective-permute-start | bytes 1572872 | tf_op jit(solution)/shard_map/ppermute | solution.py:19
  261.6 16.2 %collective-permute-start.5 = (f32[1024,128]{1,0:T(8,128)}, f32[1024,128]{1,0:T(8,128)}, u32[]{:S(2)}, u32[]{:S(2)}) collective-permute-start(f32[1024,128]{1,0:T(8,128)} %scatter_custom_fusion.6), channel_id=1, source_target_pairs={{0,1},{1,2},{2,3},{3,4},{4,5},{5,6},{6,7},{7,8},{8,9},{9,10},{10,1... | collective-permute-start | bytes 1572872 | tf_op jit(solution)/shard_map/ppermute | solution.py:19
  281.9 114.0 %reduce-scatter.17.cloned.1.call-start = ((), (), s32[]{:S(2)}) async-start(), calls=%async_computation.18 | async-start | bytes 589824 | tf_op jit(solution)/shard_map/reduce_scatter | solution.py:58
  325.5 15.9 %collective-permute-start.6 = (f32[1024,128]{1,0:T(8,128)}, f32[1024,128]{1,0:T(8,128)}, u32[]{:S(2)}, u32[]{:S(2)}) collective-permute-start(f32[1024,128]{1,0:T(8,128)} %bitcast.22), channel_id=1, source_target_pairs={{0,31},{1,0},{2,1},{3,2},{4,3},{5,4},{6,5},{7,6},{8,7},{9,8},{10,9... | collective-permute-start | bytes 1572872 | tf_op jit(solution)/shard_map/ppermute | solution.py:19
  348.8 16.2 %collective-permute-start.7 = (f32[1024,128]{1,0:T(8,128)}, f32[1024,128]{1,0:T(8,128)}, u32[]{:S(2)}, u32[]{:S(2)}) collective-permute-start(f32[1024,128]{1,0:T(8,128)} %scatter_custom_fusion.8), channel_id=1, source_target_pairs={{0,1},{1,2},{2,3},{3,4},{4,5},{5,6},{6,7},{7,8},{8,9},{9,10},{10,1... | collective-permute-start | bytes 1572872 | tf_op jit(solution)/shard_map/ppermute | solution.py:19
  368.7 189.4 %reduce-scatter.19.cloned.1.call-start = ((), (), s32[]{:S(2)}) async-start(), calls=%async_computation.19 | async-start | bytes 589824 | tf_op jit(solution)/shard_map/reduce_scatter | solution.py:58
  489.9 12.8 %collective-permute-start.8 = (f32[1024,128]{1,0:T(8,128)}, f32[1024,128]{1,0:T(8,128)}, u32[]{:S(2)}, u32[]{:S(2)}) collective-permute-start(f32[1024,128]{1,0:T(8,128)} %bitcast.24), channel_id=1, source_target_pairs={{0,31},{1,0},{2,1},{3,2},{4,3},{5,4},{6,5},{7,6},{8,7},{9,8},{10,9... | collective-permute-start | bytes 1572872 | tf_op jit(solution)/shard_map/ppermute | solution.py:19
  511.0 15.8 %collective-permute-start.9 = (f32[1024,128]{1,0:T(8,128)}, f32[1024,128]{1,0:T(8,128)}, u32[]{:S(2)}, u32[]{:S(2)}) collective-permute-start(f32[1024,128]{1,0:T(8,128)} %scatter_custom_fusion.10), channel_id=1, source_target_pairs={{0,1},{1,2},{2,3},{3,4},{4,5},{5,6},{6,7},{7,8},{8,9},{9,10},{10,1... | collective-permute-start | bytes 1572872 | tf_op jit(solution)/shard_map/ppermute | solution.py:19
  530.9 115.4 %reduce-scatter.21.cloned.1.call-start = ((), (), s32[]{:S(2)}) async-start(), calls=%async_computation.20 | async-start | bytes 589824 | tf_op jit(solution)/shard_map/reduce_scatter | solution.py:58
  574.4 16.0 %collective-permute-start.10 = (f32[1024,128]{1,0:T(8,128)}, f32[1024,128]{1,0:T(8,128)}, u32[]{:S(2)}, u32[]{:S(2)}) collective-permute-start(f32[1024,128]{1,0:T(8,128)} %bitcast.26), channel_id=1, source_target_pairs={{0,31},{1,0},{2,1},{3,2},{4,3},{5,4},{6,5},{7,6},{8,7},{9,8},{10,9... | collective-permute-start | bytes 1572872 | tf_op jit(solution)/shard_map/ppermute | solution.py:19
  598.8 16.2 %collective-permute-start.11 = (f32[1024,128]{1,0:T(8,128)}, f32[1024,128]{1,0:T(8,128)}, u32[]{:S(2)}, u32[]{:S(2)}) collective-permute-start(f32[1024,128]{1,0:T(8,128)} %scatter_custom_fusion.12), channel_id=1, source_target_pairs={{0,1},{1,2},{2,3},{3,4},{4,5},{5,6},{6,7},{7,8},{8,9},{9,10},{10,1... | collective-permute-start | bytes 1572872 | tf_op jit(solution)/shard_map/ppermute | solution.py:19
  619.0 186.7 %reduce-scatter.23.cloned.1.call-start = ((), (), s32[]{:S(2)}) async-start(), calls=%async_computation.21 | async-start | bytes 589824 | tf_op jit(solution)/shard_map/reduce_scatter | solution.py:58
  740.0 12.8 %collective-permute-start.12 = (f32[1024,128]{1,0:T(8,128)}, f32[1024,128]{1,0:T(8,128)}, u32[]{:S(2)}, u32[]{:S(2)}) collective-permute-start(f32[1024,128]{1,0:T(8,128)} %bitcast.28), channel_id=1, source_target_pairs={{0,31},{1,0},{2,1},{3,2},{4,3},{5,4},{6,5},{7,6},{8,7},{9,8},{10,9... | collective-permute-start | bytes 1572872 | tf_op jit(solution)/shard_map/ppermute | solution.py:19
  759.6 15.6 %collective-permute-start.13 = (f32[1024,128]{1,0:T(8,128)S(1)}, f32[1024,128]{1,0:T(8,128)S(1)}, u32[]{:S(2)}, u32[]{:S(2)}) collective-permute-start(f32[1024,128]{1,0:T(8,128)S(1)} %scatter_custom_fusion.14), channel_id=1, source_target_pairs={{0,1},{1,2},{2,3},{3,4},{4,5},{5,6},{6,7},{7,8},{8,9},{9,10},{10,1... | collective-permute-start | bytes 1572872 | tf_op jit(solution)/shard_map/ppermute | solution.py:19
  898.3 12.4 %collective-permute-start.14 = (f32[1024,128]{1,0:T(8,128)S(1)}, f32[1024,128]{1,0:T(8,128)S(1)}, u32[]{:S(2)}, u32[]{:S(2)}) collective-permute-start(f32[1024,128]{1,0:T(8,128)S(1)} %bitcast.70), channel_id=1, source_target_pairs={{0,31},{1,0},{2,1},{3,2},{4,3},{5,4},{6,5},{7,6},{8,7},{9,8},{10,9... | collective-permute-start | bytes 1572872 | tf_op jit(solution)/shard_map/ppermute | solution.py:19
  (12 other events, 528.0 us)
Sparse Core Ops, SparseCore 0:
  61.3 31.2 reduce-scatter.24
  95.0 32.6 reduce-scatter.10
  194.1 27.0 reduce-scatter.12
  282.0 27.0 reduce-scatter.14
  368.8 27.0 reduce-scatter.16
  531.0 27.0 reduce-scatter.18
  619.2 27.0 reduce-scatter.20
  778.6 27.0 reduce-scatter.22
